TPU v7x, 128 devices: a whole 4x4x4 slice. The times are simulated.
128 devices in a mesh: dp: 32 (over y_lo, z, x), tensor: 4 (over y_hi, core).
Axes of the slice: x: 4, y: 4 (y_hi: 2, y_lo: 2; y = y_hi * 2 + y_lo), z: 4, core: 2. Of those that a mesh axis runs over, the one named last changes fastest.
Arguments:
- tokens_in: bfloat16 [16384, 2048], P(('dp', 'tensor')), may hold values from -6 to 6
- cotangent: bfloat16 [16384, 2048], P(('dp', 'tensor')), may hold values from -6 to 6
- seq_ids: int32 [16384], P('dp'), may hold values from 0 to 1, as said below
- block_ids: int32 [16384], P('dp'), may hold values from 0 to 1, as said below
- positions: int32 [16384], P('dp'), may hold values from 0 to 383, as said below
- attn_gain: bfloat16 [2048], P('dp'), may hold values from 0.5 to 1.5
- ffn_gain: bfloat16 [2048], P('dp'), may hold values from 0.5 to 1.5
- w_query: bfloat16 [2048, 2048], P('dp', 'tensor'), may hold values from -0.125 to 0.125
- w_key: bfloat16 [2048, 256], P('dp', 'tensor'), may hold values from -0.125 to 0.125
- w_value: bfloat16 [2048, 256], P('dp', 'tensor'), may hold values from -0.125 to 0.125
- w_out: bfloat16 [2048, 2048], P('tensor', 'dp'), may hold values from -1 to 1
- w_gate: bfloat16 [2048, 5632], P('dp', 'tensor'), may hold values from -0.125 to 0.125
- w_up: bfloat16 [2048, 5632], P('dp', 'tensor'), may hold values from -0.125 to 0.125
- w_down: bfloat16 [5632, 2048], P('tensor', 'dp'), may hold values from -0.15625 to 0.15625
Outputs:
- result: bfloat16 [16384, 2048], P(('dp', 'tensor'))
- grad_tokens: bfloat16 [16384, 2048], P(('dp', 'tensor'))
- grad_attn_gain: float32 [2048], P('dp')
- grad_ffn_gain: float32 [2048], P('dp')
- grad_w_query: float32 [2048, 2048], P('dp', 'tensor')
- grad_w_key: float32 [2048, 256], P('dp', 'tensor')
- grad_w_value: float32 [2048, 256], P('dp', 'tensor')
- grad_w_out: float32 [2048, 2048], P('tensor', 'dp')
- grad_w_gate: float32 [2048, 5632], P('dp', 'tensor')
- grad_w_up: float32 [2048, 5632], P('dp', 'tensor')
- grad_w_down: float32 [5632, 2048], P('tensor', 'dp')
Inputs may be any that keep to these rules, and one draw needn't show every extreme that they name: `seq_ids`: each run of 512 tokens holds two documents, 0 then 1, each of 128 to 384 tokens; never falls within a run. `positions`: counted from 0 at the start of each document; some document has 384 tokens. `block_ids`: the attention block of the token's place in its document, of 256 places each; some document has 384 tokens.
All inputs are finite; a program needn't handle non-finite values.
Results may differ from a plain program's by a relative error of at most 0.03.
Values may be sent and summed in bfloat16 or wider, within the bound.
A program may use at most 128 MiB of HBM per device.

v0:
```python
import functools
import math

import jax
import jax.numpy as jnp
import numpy as np
from jax import lax
from jax.experimental import pallas as pl
from jax.experimental.pallas import tpu as pltpu
from jax.sharding import PartitionSpec as P

HD = 64
EPSILON = 1e-05
ROPE_BASE = 10000.0
MESH = pl.DeviceIdType.MESH
BF = jnp.bfloat16
F32 = jnp.float32
ANY = pl.BlockSpec(memory_space=pl.ANY)
VM = pl.BlockSpec(memory_space=pltpu.VMEM)
FH = 768


class Net:
    def __init__(self, send, recv, loc):
        self.send, self.recv, self.loc = send, recv, loc
        self.n = self.m = 0
        dp, t = lax.axis_index("dp"), lax.axis_index("tensor")
        self.a = lax.div(dp, 16)
        self.z = lax.rem(lax.div(dp, 4), 4)
        self.x = lax.rem(dp, 4)
        self.hi = lax.div(t, 2)
        self.c = lax.rem(t, 2)
        self.t = t
        self.sends = []

    def dev(self, a=None, z=None, x=None, hi=None, c=None):
        a = self.a if a is None else a
        z = self.z if z is None else z
        x = self.x if x is None else x
        hi = self.hi if hi is None else hi
        c = self.c if c is None else c
        return (a * 16 + z * 4 + x, hi * 2 + c)

    def xp(self, s):
        return self.dev(x=lax.rem(self.x + s, 4))

    def zp(self, s):
        return self.dev(z=lax.rem(self.z + s, 4))

    def first(self, s, own):
        k = self.a if own else 1 - self.a
        return self.dev(z=lax.rem(self.z + s * k, 4), x=lax.rem(self.x + s * (1 - k), 4))

    def flip(self, da, dh):
        return self.dev(a=1 - self.a if da else None, hi=1 - self.hi if dh else None)

    def ring(self, s):
        a, hi = self.a, self.hi
        k = a if s == 1 else 1 - a
        return (a, 1 - hi) if s == 2 else (1 - a, hi + k - 2 * hi * k)

    def yp(self, s):
        a, hi = self.ring(s)
        return self.dev(a=a, hi=hi)

    def sib(self):
        return self.dev(c=1 - self.c)

    def hello(self, peers):
        bar = pltpu.get_barrier_semaphore()
        for p in peers:
            pl.semaphore_signal(bar, inc=1, device_id=p, device_id_type=MESH)

    def met(self, peers):
        pl.semaphore_wait(pltpu.get_barrier_semaphore(), len(peers))

    def greet(self, peers):
        self.hello(peers)
        self.met(peers)

    def put(self, src, dst, dev):
        i = self.n
        self.n += 1
        cp = pltpu.make_async_remote_copy(
            src_ref=src, dst_ref=dst, send_sem=self.send.at[i], recv_sem=self.recv.at[i],
            device_id=dev, device_id_type=MESH,
        )
        cp.start()
        self.sends.append(cp)
        return cp

    def copy(self, src, dst):
        i = self.m
        self.m += 1
        cp = pltpu.make_async_copy(src, dst, self.loc.at[i])
        cp.start()
        return cp

    def drop(self, cp):
        self.sends = [s for s in self.sends if s is not cp]

    def finish(self):
        assert self.n <= self.send.shape[0] and self.m <= self.loc.shape[0]
        for cp in self.sends:
            cp.wait_send()


FLIP8 = ((1, 0), (1, 1), (0, 1))
ORDER = (1, 3, 2)


def sems(n, m):
    return [pltpu.SemaphoreType.DMA((n,)), pltpu.SemaphoreType.DMA((n,)), pltpu.SemaphoreType.DMA((m,))]


def all_peers(net):
    return (
        [net.xp(s) for s in ORDER]
        + [net.zp(s) for s in ORDER]
        + [net.sib()]
        + [net.flip(*f) for f in FLIP8]
    )


def rms_unit(u):
    return lax.rsqrt(jnp.mean(u * u, -1, keepdims=True) + EPSILON)


def add_to(dst, terms, rows, step=32):
    @pl.loop(0, rows // step)
    def _(i):
        sl = pl.ds(pl.multiple_of(i * step, step), step)
        total = terms[0][sl, :].astype(F32)
        for ref in terms[1:]:
            total += ref[sl, :].astype(F32)
        dst[sl, :] = total.astype(dst.dtype)


def dot(l, r, dims=((1,), (0,))):
    return lax.dot_general(l, r, (dims, ((), ())), preferred_element_type=F32)


NT = ((1,), (1,))
TN = ((0,), (0,))


def low_half(shape):
    return lax.broadcasted_iota(jnp.int32, shape, 1) < HD


def first_quarter(shape):
    lane = lax.broadcasted_iota(jnp.int32, shape, 1)
    return lax.rem(lane, HD) < HD // 2


def rot(u, cos, sin):
    near = jnp.where(first_quarter(u.shape), pltpu.roll(u, 96, 1), pltpu.roll(u, 32, 1))
    return u * cos + near * sin


def rot_back(w, cos, sin):
    y = w * sin
    near = jnp.where(first_quarter(w.shape), pltpu.roll(y, 96, 1), pltpu.roll(y, 32, 1))
    return w * cos + near


class Gather:
    def __init__(self, net, src, dst, half):
        self.net, self.dst = net, dst
        self.own = src.at[net.a] if half else src
        self.other = src.at[1 - net.a] if half else src
        self.here = dst.at[net.a, net.z, net.x]

    def local(self):
        self.lc = self.net.copy(self.own, self.here)

    def over_y(self):
        self.yc = self.net.put(self.other, self.here, self.net.flip(1, 0))

    def stage_own(self):
        self.st = [self.net.put(self.own, self.here, self.net.first(s, True)) for s in ORDER]

    def stage_other(self):
        net = self.net
        self.yc.wait_recv()
        there = self.dst.at[1 - net.a, net.z, net.x]
        self.st += [net.put(there, there, net.first(s, False)) for s in ORDER]

    def stage_two(self):
        net, dst = self.net, self.dst
        self.lc.wait()
        for cp in self.st:
            cp.wait_recv()
        z, x = net.z, net.x
        self.near = [
            (net.put(dst.at[0, z], dst.at[0, z], net.zp(s)), net.put(dst.at[1, :, x], dst.at[1, :, x], net.xp(s)))
            for s in (1, 3)
        ]

    def forward(self):
        net, dst = self.net, self.dst
        self.last = []
        for (cz, cx), s, lo in zip(self.near, (1, 3), (0, 2)):
            cz.wait_recv()
            blk = dst.at[0, lax.rem(net.z + 4 - s, 4), lo : lo + 2]
            self.last.append(net.put(blk, blk, net.zp(s)))
            cx.wait_recv()
            blk = dst.at[1, lo : lo + 2, lax.rem(net.x + 4 - s, 4)]
            self.last.append(net.put(blk, blk, net.xp(s)))

    def done(self):
        for cp in self.last:
            cp.wait_recv()


class Rows8:
    def __init__(self, net, mine, dst):
        self.net, self.dst, self.half = net, dst, mine.shape[0] // 2
        at = dst.at[net.a, net.t]
        self.up, self.down = net.put(mine, at, net.yp(1)), net.put(mine, at, net.yp(3))
        self.side = [net.put(mine, at, net.sib())]

    def at(self, s):
        a, hi = self.net.ring(s)
        return self.dst.at[a, hi * 2 + self.net.c]

    def forward(self):
        net, h = self.net, self.half
        self.last = []
        for cp, src, to, lo in ((self.up, 3, 1, 0), (self.down, 1, 3, h)):
            cp.wait_recv()
            blk = self.at(src)
            part = blk.at[lo : lo + h]
            self.last.append(net.put(part, part, net.yp(to)))
            self.side.append(net.put(blk, blk, net.sib()))

    def finish(self):
        for cp in self.last:
            cp.wait_recv()
        blk = self.at(2)
        self.side.append(self.net.put(blk, blk, self.net.sib()))

    def done(self):
        for cp in self.side:
            cp.wait_recv()


def pack_halves(dst, w):
    rest = w.shape[1] - FH
    dst[0] = w[:, :FH]
    dst[1, :, :rest] = w[:, FH:]
    dst[1, :, rest:] = jnp.zeros((w.shape[0], FH - rest), BF)


def column(row, n):
    return jnp.broadcast_to(row, (128, n)).T


def m1_body(
    tok, cot, w_q, w_k, w_v, wo, w_g, w_u, w_d, g_a, g_f, freq, seqr, blkr, posr,
    xf, mid, gains, h_xn, h_q, h_kv4, h_att, h_aq, h_ao, h_cos, h_sin, h_bias_t, cot_all, ag, au, ad,
    xn, q, kv4, att, aq, ao, cos, sin, bias_t, wq, wf, gn, tall, an, bias, ones2, part, rc, rh, send, recv, loc,
):
    net = Net(send, recv, loc)
    a, z, x, t, hi, c = net.a, net.z, net.x, net.t, net.hi, net.c
    rows, d = tok.shape
    n = 4 * rows
    nq = w_q.shape[1]
    net.hello(all_peers(net))
    lane = lax.broadcasted_iota(jnp.int32, (1, 128), 1)
    here = lax.div(lane, HD) == lax.rem(x, 2)
    gn[...] = jnp.zeros_like(gn)
    for i, g in enumerate((g_a, g_f)):
        g = g[...].astype(F32)
        gn[i : i + 1, :] = jnp.where(here, jnp.concatenate([g, g], 1), 0.0)
    wq[:, :nq] = w_q[...]
    wq[:, nq : nq + HD] = w_k[...]
    wq[:, nq + HD :] = w_v[...]
    net.met(all_peers(net))
    far, near = 1 - hi, hi
    tt = far * 2 + c
    sib, chip = net.sib(), net.flip(0, 1)
    tl = net.copy(tok, tall.at[t])
    tf = net.put(tok, tall.at[t], chip)
    ts = [net.put(tok, tall.at[t], sib)]
    gg, gq, go = Gather(net, gn, an, False), Gather(net, wq, aq, False), Gather(net, wo, ao, False)
    for g in (gg, gq, go):
        g.over_y()
        g.local()
        g.stage_own()
    cl = net.copy(cot, cot_all.at[a, t])
    for i, w in enumerate((w_g, w_u, w_d)):
        pack_halves(wf.at[i], w)
    ffn = [Gather(net, wf.at[i], o, True) for i, o in enumerate((ag, au, ad))]
    for g in ffn:
        g.local()
    for g in (gg, gq, go):
        g.stage_other()
    seq, blk = seqr[...].astype(F32), blkr[...].astype(F32)
    same = column(seq, n)[:, :1] == seq
    blkc = column(blk, n)[:, :1]
    bias[...] = jnp.where(same & (blk <= blkc), jnp.float32(0.0), jnp.float32(-1e30))
    bias_t[...] = jnp.where(same & (blkc <= blk), jnp.float32(0.0), jnp.float32(-1e30))
    for g in (gg, gq, go):
        g.stage_two()
    tf.wait_recv()
    ts.append(net.put(tall.at[tt], tall.at[tt], sib))
    for g in ffn:
        g.over_y()
    cots = Rows8(net, cot, cot_all)
    angles = column(posr[...].astype(F32), n) * freq[...]
    cos[...] = jnp.cos(angles)
    sine = jnp.sin(angles)
    sin[...] = jnp.where(first_quarter(sine.shape), -sine, sine)
    tl.wait()
    for cp in ts:
        cp.wait_recv()
    gg.forward()
    gq.forward()
    out = [net.copy(*p) for p in ((bias_t, h_bias_t), (cos, h_cos), (sin, h_sin))]
    gg.done()
    for i in range(16):
        k = 2 * i
        pair = an[k // 16, k // 4 % 4, k % 4] + an[k // 16, k // 4 % 4, k % 4 + 1]
        gains[:, 128 * i : 128 * i + 128] = pair
    step = 32

    @pl.loop(0, n // step)
    def _(i):
        b = lax.div(i, rows // step)
        u = tall[b, pl.ds(pl.multiple_of(lax.rem(i, rows // step) * step, step), step), :].astype(F32)
        xn[pl.ds(pl.multiple_of(i * step, step), step), :] = (u * rms_unit(u) * gains[0:1, :]).astype(BF)

    go.forward()
    gq.done()
    for g in ffn:
        g.stage_own()
    scale = 1.0 / math.sqrt(HD)
    for lo, width in ((0, 256), (256, 256), (512, 128)):
        w = aq[:, :, :, :, lo : lo + width].reshape(d, width)
        val = dot(xn[...], w)
        if lo < 512:
            for i in range(2):
                at = lo + 128 * i
                q[:, at : at + 128] = (rot(val[:, 128 * i : 128 * i + 128], cos[...], sin[...]) * scale).astype(BF)
        else:
            low = low_half(val.shape)
            ke = jnp.where(low, rot(val, cos[...], sin[...]), 0.0)
            vo = jnp.where(low, 0.0, val)
            ve = pltpu.roll(vo, 64, 1)
            kv4[0] = ke.astype(BF)
            kv4[1] = pltpu.roll(ke, 64, 1).astype(BF)
            kv4[2] = ve.astype(BF)
            kv4[3] = vo.astype(BF)
            ones2[0] = jnp.where(low, ve, 1.0).astype(BF)
            ones2[1] = jnp.where(low, 1.0, vo).astype(BF)
    for g in ffn:
        g.stage_other()

    @pl.loop(0, 4)
    def _(j):
        ln = pl.ds(pl.multiple_of(j * 128, 128), 128)
        qp = q[:, ln]
        low = low_half((n, 128))
        o = []
        for h in range(2):
            s = dot(qp, kv4[h], NT) + bias[...]
            e = jnp.exp(s - jnp.max(s, -1, keepdims=True)).astype(BF)
            o.append(dot(e, ones2[h]))
        total = jnp.where(low, pltpu.roll(o[0], 64, 1), pltpu.roll(o[1], 64, 1))
        att[:, ln] = (jnp.where(low, o[0], o[1]) / total).astype(BF)

    go.done()
    for i in range(4):
        w = ao[i // 2, 2 * (i % 2) : 2 * (i % 2) + 2].reshape(512, 512)
        part[:, :, 512 * i : 512 * i + 512] = dot(att[...], w, NT).reshape(4, rows, 512).astype(BF)
    out += [
        net.copy(*p)
        for p in ((xn, h_xn), (q, h_q), (kv4, h_kv4), (att, h_att), (aq, h_aq), (ao, h_ao))
    ]
    cc = [net.put(part.at[h * 2 + (1 - c)], rc.at[i], sib) for i, h in enumerate((far, near))]
    for g in ffn:
        g.stage_two()
    cc[0].wait_recv()
    pf = part.at[far * 2 + c]
    add_to(pf, [pf, rc.at[0]], rows)
    ch = net.put(pf, rh, chip)
    cots.forward()
    cc[1].wait_recv()
    ch.wait_recv()
    ffn[0].forward()
    mine_part = part.at[near * 2 + c]

    @pl.loop(0, rows // step)
    def _(i):
        sl = pl.ds(pl.multiple_of(i * step, step), step)
        m = (
            tall[t, sl, :].astype(F32)
            + (mine_part[sl, :].astype(F32) + rc[1, sl, :].astype(F32))
            + rh[sl, :].astype(F32)
        )
        mid[sl, :] = m
        xf[a, t, sl, :] = (m * rms_unit(m) * gains[1:2, :]).astype(BF)

    mine = xf.at[a, t]
    rows8 = Rows8(net, mine, xf)
    cots.finish()
    ffn[1].forward()
    rows8.forward()
    ffn[2].forward()
    rows8.finish()
    for cp in [cl] + out:
        cp.wait()
    for g in ffn:
        g.done()
    cots.done()
    rows8.done()
    net.finish()


def m1(tok, cot, weights, g_a, g_f, seq, blk, pos):
    rows, d = tok.shape
    n = 4 * rows
    sd = jax.ShapeDtypeStruct
    v = pltpu.VMEM
    row = lambda u: u.reshape(1, n)
    freq = 1.0 / ROPE_BASE ** (np.arange(HD // 2, dtype=np.float32) * 2.0 / HD)
    freq = jnp.asarray(np.tile(freq, 4)[None], F32)
    ffn = [sd((2, 4, 4, 64, FH), BF)] * 3
    kept = [
        ((n, d), BF), ((n, 512), BF), ((4, n, 128), BF), ((n, 512), BF), ((2, 4, 4, 64, 640), BF),
        ((2, 4, 4, 64, 512), BF), ((n, 128), F32), ((n, 128), F32), ((n, n), F32),
    ]
    return pl.pallas_call(
        m1_body,
        out_shape=[sd((2, 4, rows, d), BF), sd((rows, d), F32), sd((8, d), F32)]
        + [sd(*k) for k in kept] + [sd((2, 4, rows, d), BF)] + ffn,
        in_specs=[ANY] * 2 + [VM] * 13,
        out_specs=[VM] * 3 + [ANY] * 13,
        scratch_shapes=[v(*k) for k in kept] + [
            v((64, 640), BF), v((3, 2, 64, FH), BF), v((8, 128), F32),
            v((4, rows, d), BF), v((2, 4, 4, 8, 128), F32), v((n, n), F32),
            v((2, n, 128), BF), v((4, rows, d), BF), v((2, rows, d), BF), v((rows, d), BF),
        ] + sems(124, 24),
        compiler_params=pltpu.CompilerParams(collective_id=1, has_side_effects=True, vmem_limit_bytes=56 << 20),
        name="attention_forward",
    )(tok, cot, *weights, g_a, g_f, freq, row(seq), row(blk), row(pos))


def add_blocks(dst, terms, blocks):
    @pl.loop(0, blocks)
    def _(b):
        total = terms[0][b].astype(F32)
        for ref in terms[1:]:
            total += ref[b].astype(F32)
        dst[b] = total.astype(dst.dtype)


class Sum8:
    def __init__(self, net, part, ploc, rc, thru, ry):
        self.net, self.ploc, self.rc, self.thru, self.ry = net, ploc, rc, thru, ry
        c = net.c
        chips = [net.ring(s) for s in (2, 1, 3)] + [(net.a, net.hi)]
        self.cc = [net.put(part.at[b, h * 2 + (1 - c)], rc.at[i], net.sib()) for i, (b, h) in enumerate(chips)]
        self.lc = [net.copy(part.at[b, h * 2 + c], ploc.at[i]) for i, (b, h) in enumerate(chips)]

    def send(self):
        net, ploc, thru, ry = self.net, self.ploc, self.thru, self.ry
        rows = ploc.shape[1]
        h = rows // 2

        def ready(i):
            self.lc[i].wait()
            self.cc[i].wait_recv()
            if i < 3:
                add_to(ploc.at[i], [ploc.at[i], self.rc.at[i]], rows)

        ready(0)
        self.far = [
            net.put(ploc.at[0, 0:h], thru.at[0], net.yp(1)), net.put(ploc.at[0, h:rows], thru.at[1], net.yp(3)),
        ]
        ready(1)
        self.near = [net.put(ploc.at[1, h:rows], ry.at[0, h:rows], net.yp(1))]
        ready(2)
        self.near.append(net.put(ploc.at[2, 0:h], ry.at[1, 0:h], net.yp(3)))
        ready(3)

    def mid(self):
        net, ploc, thru, ry = self.net, self.ploc, self.thru, self.ry
        h = ploc.shape[1] // 2
        for k, (to, lo) in enumerate(((1, 0), (3, h))):
            self.far[k].wait_recv()
            part = ploc.at[1 + k, lo : lo + h]
            add_to(part, [part, thru.at[k]], h)
            self.near.append(net.put(part, ry.at[k, lo : lo + h], net.yp(to)))

    def arrived(self):
        for cp in self.near:
            cp.wait_recv()

    def drained(self):
        for cp in self.far + self.near:
            cp.wait_send()
            self.net.drop(cp)

    def rows(self, sl):
        total = self.ploc[3, sl, :].astype(F32) + self.rc[3, sl, :].astype(F32)
        for j in range(2):
            total += self.ry[j, sl, :].astype(F32)
        return total


def norm_back(u, g, gain):
    r = rms_unit(u)
    unit = u * r
    gvec = g * gain
    return r * (gvec - unit * jnp.mean(gvec * unit, -1, keepdims=True))


class Scatter:
    def __init__(self, net, part, thru, r1, r2, loc=None):
        self.net, self.part, self.thru, self.r1, self.r2, self.loc = net, part, thru, r1, r2, loc

    def block(self, h, s):
        p, net = self.part, self.net
        if h == 0:
            zz = lax.rem(net.z + s, 4)
            return lambda lo, hi: p.at[0, zz, lo:hi]
        xx = lax.rem(net.x + s, 4)
        return lambda lo, hi: p.at[1, lo:hi, xx]

    def stage_one(self):
        net, r1, thru = self.net, self.r1, self.thru
        self.got, self.lc, self.add = [], [], []
        for h in range(2):
            to = net.zp if h == 0 else net.xp
            far, up, down, own = (self.block(h, s) for s in (2, 1, 3, 0))
            self.got.append([
                net.put(far(0, 2), thru.at[h, 0], to(1)), net.put(far(2, 4), thru.at[h, 1], to(3)),
                net.put(up(2, 4), r1.at[h, 0, 2:4], to(1)), net.put(down(0, 2), r1.at[h, 1, 0:2], to(3)),
            ])
            if self.loc is None:
                self.lc.append([])
                self.add.append((up(0, 2), down(2, 4), own(0, 4)))
            else:
                l = self.loc
                self.add.append((l.at[h, 0:2], l.at[h, 2:4], l.at[h, 4:8]))
                self.lc.append([net.copy(f, t) for f, t in zip((up(0, 2), down(2, 4), own(0, 4)), self.add[h])])

    def stage_mid(self):
        net, r1, thru = self.net, self.r1, self.thru
        self.more = []
        for h in range(2):
            to = net.zp if h == 0 else net.xp
            for cp in self.lc[h]:
                cp.wait()
            for k, s in enumerate((1, 3)):
                self.got[h][k].wait_recv()
                add_blocks(thru.at[h, k], [thru.at[h, k], self.add[h][k]], 2)
                self.more.append(net.put(thru.at[h, k], r1.at[h, k, 2 * k : 2 * k + 2], to(s)))

    def stage_two(self):
        net, r1, r2 = self.net, self.r1, self.r2
        self.nxt = []
        for h in range(2):
            for cp in self.got[h][2:] + self.more[2 * h : 2 * h + 2]:
                cp.wait_recv()
            add_blocks(r1.at[h, 0], [self.add[h][2], r1.at[h, 0], r1.at[h, 1]], 4)
            me = net.x if h == 0 else net.z
            self.nxt.append([
                net.put(r1.at[h, 0, lax.rem(me + s, 4)], r2.at[h, k], net.xp(s) if h == 0 else net.zp(s))
                for k, s in enumerate(ORDER)
            ])

    def stage_y(self, dst):
        net, r1, r2 = self.net, self.r1, self.r2
        for h in range(2):
            for cp in self.nxt[h]:
                cp.wait_recv()
            me = net.x if h == 0 else net.z
            add_to(r2.at[h, 0], [r1.at[h, 0, me]] + [r2.at[h, k] for k in range(3)], 64)
        self.yc = net.put(r2.at[1 - net.a, 0], dst, net.flip(1, 0))


def weight_grads(left, pairs, chunk, stage, csem, ssem):
    n = len(pairs)

    def load(i, k):
        sl = pl.ds(pl.multiple_of(i * 256, 256), 256)
        return pltpu.make_async_copy(left.at[:, sl], chunk.at[k], csem.at[k])

    def save(i, w, k):
        return pltpu.make_async_copy(stage.at[k], pairs[w][1].at[lax.div(i, 4), lax.rem(i, 4)], ssem.at[k])

    for i in range(3):
        load(i, i).start()

    @pl.loop(0, 2)
    def _(j):
        for k in range(4):
            i = 4 * j + k
            load(i, k).wait()
            if k == 0:
                load(i + 3, 3).start()
            else:

                @pl.when(j < 1)
                def _():
                    load(i + 3, k - 1).start()

            for w in range(n):
                slot = n * (k % 2) + w
                if k > 1:
                    save(i - 2, w, slot).wait()
                else:

                    @pl.when(j > 0)
                    def _():
                        save(i - 2, w, slot).wait()

                stage[slot] = dot(chunk[k], pairs[w][0][...], TN).reshape(4, 64, FH).astype(BF)
                save(i, w, slot).start()

    for i in (6, 7):
        for w in range(n):
            save(i, w, n * (i % 2) + w).wait()


SOON = ("hid", "dgate", "dup")
LATE = SOON + ("xn", "q", "kv4", "att", "wq", "wo", "cos", "sin", "bias", "tok", "w_q", "w_k", "w_v", "w_g", "w_u")


def m3_body(names, *refs):
    r = dict(zip(names, refs))
    net = Net(r["send"], r["recv"], r["loc"])
    a, z, x, t, hi, c = net.a, net.z, net.x, net.t, net.hi, net.c
    diag = net.dev(hi=1 - net.hi, c=1 - net.c)
    net.greet(all_peers(net) + [diag])
    mid, cot, tok, gains = r["mid"], r["cot"], r["tok"], r["gains"]
    rows, d = cot.shape
    n = 4 * rows
    step = 32
    far, near = 1 - hi, hi
    sib, chip = net.sib(), net.flip(0, 1)
    bl, bc, bt, by = r["bl"], r["bc"], r["bt"], r["by"]
    late = [net.copy(r["h_" + k], r[k]) for k in LATE if k not in SOON]
    soon = [net.copy(r["h_" + k], r[k]) for k in SOON]
    back = Sum8(net, r["fback"], bl, bc, bt, by)
    bias = r["bias"]
    ffn = [Scatter(net, r["p" + k], r["t" + k], r["r1" + k], r["r2" + k], r["l" + k]) for k in "dgu"]
    work = (r["chunk"], r["stage"], r["csem"], r["ssem"])
    soon[0].wait()
    weight_grads(r["call"], [(r["hid"], r["pd"])], *work)
    back.send()
    ffn[0].stage_one()
    soon[1].wait()
    soon[2].wait()
    weight_grads(r["xf"], [(r["dgate"], r["pg"]), (r["dup"], r["pu"])], *work)
    back.mid()
    ffn[1].stage_one()
    ffn[2].stage_one()
    back.arrived()
    gm, gmid = r["gm"], r["gmid"]

    @pl.loop(0, rows // step)
    def _(i):
        sl = pl.ds(pl.multiple_of(i * step, step), step)
        g = back.rows(sl)
        m = cot[sl, :].astype(F32) + norm_back(mid[sl, :], g, gains[1:2, :])
        gmid[sl, :] = m
        gm[t, sl, :] = m.astype(BF)

    free = r["free"]
    for s in (1, 3):
        pl.semaphore_signal(free, inc=1, device_id=net.yp(s), device_id_type=MESH)
    mine = gm.at[t]
    mf = net.put(mine, mine, chip)
    ms = [net.put(mine, mine, sib)]
    ffn[0].stage_mid()
    ms[0].wait_recv()
    back.drained()
    fwd = Sum8(net, r["fout"], bl, bc, bt, by)
    pl.semaphore_wait(free, 2)
    mf.wait_recv()
    theirs = gm.at[far * 2 + c]
    ms.append(net.put(theirs, theirs, sib))
    fwd.send()
    ffn[1].stage_mid()
    ms[1].wait_recv()
    for cp in late:
        cp.wait()
    gatt, att, q, kv4, wq, wo = r["gatt"], r["att"], r["q"], r["kv4"], r["wq"], r["wo"]
    for i in range(2):
        w = wo[:, :, :, :, 256 * i : 256 * i + 256].reshape(d, 256)
        gatt[:, 256 * i : 256 * i + 256] = dot(gm[...].reshape(n, d), w).astype(BF)
    po, pq, xn, dqkv = r["po"], r["pq"], r["xn"], r["dqkv"]

    @pl.loop(0, 8)
    def _(i):
        ln = pl.ds(pl.multiple_of(i * 256, 256), 256)
        left = gm[:, :, ln].reshape(n, 256)
        po[lax.div(i, 4), lax.rem(i, 4)] = dot(left, att[...], TN).reshape(4, 64, 512).astype(BF)

    so = Scatter(net, po, r["to"], r["r1o"], r["r2o"])
    so.stage_one()
    ffn[2].stage_mid()
    ak, av = r["ak"], r["av"]
    ak[...] = jnp.zeros_like(ak)
    av[...] = jnp.zeros_like(av)
    cos, sin = r["cos"], r["sin"]
    low = low_half((n, 128))
    scale = 1.0 / math.sqrt(HD)

    def pair(j):
        ln = pl.ds(pl.multiple_of(j * 128, 128), 128)
        qp, gp = q[:, ln], gatt[:, ln]
        cv, ck, gq = [], [], None
        for h in range(2):
            s = dot(kv4[h], qp, NT) + bias[...]
            e = jnp.exp(s - jnp.max(s, 0, keepdims=True))
            p = e * (1.0 / jnp.sum(e, 0, keepdims=True))
            pg = p * dot(kv4[2 + h], gp, NT)
            graw = (pg - p * jnp.sum(pg, 0, keepdims=True)).astype(BF)
            cv.append(dot(p.astype(BF), gp))
            ck.append(dot(graw, qp))
            term = dot(kv4[h], graw, TN)
            gq = term if gq is None else gq + term
        av[...] += jnp.where(low, cv[0], cv[1])
        ak[...] += jnp.where(low, ck[0], ck[1])
        dqkv[:, ln] = (rot_back(gq.T, cos[...], sin[...]) * scale).astype(BF)

    fwd.mid()
    ffn[0].stage_two()
    ffn[1].stage_two()
    pl.loop(0, 4)(pair)
    so.stage_mid()
    tk = ak[...] + pltpu.roll(ak[...], 64, 1)
    tv = av[...] + pltpu.roll(av[...], 64, 1)
    dqkv[:, 512:640] = jnp.where(low, rot_back(tk, cos[...], sin[...]), tv).astype(BF)


    def settle(i):
        o = r["y" + "dgu"[i]]
        ffn[i].stage_y(o.at[a])
        o[a] = ffn[i].r2[a, 0]

    ap, arc, arh = r["ap"], r["arc"], r["arh"]
    for i in range(4):
        w = wq[i // 2, 2 * (i % 2) : 2 * (i % 2) + 2].reshape(512, 640)
        ap[:, :, 512 * i : 512 * i + 512] = dot(dqkv[...], w, NT).reshape(4, rows, 512).astype(BF)
    acc = [net.put(ap.at[h * 2 + (1 - c)], arc.at[i], sib) for i, h in enumerate((far, near))]

    @pl.loop(0, 8)
    def _(i):
        ln = pl.ds(pl.multiple_of(i * 256, 256), 256)
        pq[lax.div(i, 4), lax.rem(i, 4)] = dot(xn[:, ln], dqkv[...], TN).reshape(4, 64, 640).astype(BF)

    sq = Scatter(net, pq, r["tq"], r["r1q"], r["r2q"])
    sq.stage_one()
    acc[0].wait_recv()
    af = ap.at[far * 2 + c]
    add_to(af, [af, arc.at[0]], rows)
    ach = net.put(af, arh, chip)
    ffn[2].stage_two()
    sq.stage_mid()
    so.stage_two()
    for i in range(3):
        settle(i)
    fwd.arrived()
    res, gtok = r["res"], r["gtok"]

    @pl.loop(0, rows // step)
    def _(i):
        sl = pl.ds(pl.multiple_of(i * step, step), step)
        g = fwd.rows(sl)
        res[sl, :] = (mid[sl, :] + g).astype(BF)

    dg = r["dg"]
    for sc in ffn:
        sc.yc.wait_recv()
    tot = jnp.zeros((64, 128), F32)
    for k in "gu":
        y, w = r["y" + k], r["w_" + k]
        for i in range(w.shape[1] // 128):
            lo, half = 128 * i % FH, 128 * i // FH
            tot += y[half, :, lo : lo + 128].astype(F32) * w[:, 128 * i : 128 * i + 128].astype(F32)
    dg[1] = tot
    sq.stage_two()
    so.stage_y(r["yo"])
    acc[1].wait_recv()
    ach.wait_recv()
    an = ap.at[near * 2 + c]

    @pl.loop(0, rows // step)
    def _(i):
        sl = pl.ds(pl.multiple_of(i * step, step), step)
        g = an[sl, :].astype(F32) + arc[1, sl, :].astype(F32) + arh[sl, :].astype(F32)
        gtok[sl, :] = (gmid[sl, :] + norm_back(tok[sl, :].astype(F32), g, gains[0:1, :])).astype(BF)

    sq.stage_y(r["yq"])
    so.yc.wait_recv()
    add_to(r["oo"], [so.r2.at[a, 0], r["yo"]], 64)
    sq.yc.wait_recv()
    dw = sq.r2[a, 0].astype(F32) + r["yq"][...].astype(F32)
    nq = r["oq"].shape[1]
    dk, dv = dw[:, nq : nq + HD], dw[:, nq + HD :]
    r["oq"][...] = dw[:, :nq]
    r["ok"][...] = dk
    r["ov"][...] = dv
    tot = jnp.zeros((64, 128), F32)
    for i in range(nq // 128):
        sl = slice(128 * i, 128 * i + 128)
        tot += dw[:, sl] * r["w_q"][:, sl].astype(F32)
    small = dk * r["w_k"][...].astype(F32) + dv * r["w_v"][...].astype(F32)
    dg[0] = tot + jnp.concatenate([small, jnp.zeros_like(small)], 1)
    dy = r["dy"]
    sums = [net.put(dg, dy.at[at], peer) for at, peer in enumerate((sib, chip, diag))]
    for cp in sums:
        cp.wait_recv()
    for i, (o, g) in enumerate((("dg1", "g_a"), ("dg2", "g_f"))):
        r[o][...] = jnp.sum((dg[i] + dy[0, i] + dy[1, i] + dy[2, i]).T, 0, keepdims=True) / r[g][...].astype(F32)
    net.finish()


def m3(hbm, vmem, shapes):
    rows, d = shapes
    n = 4 * rows
    sd = jax.ShapeDtypeStruct
    v = pltpu.VMEM
    part = (2, 4, 4, 64, FH)
    outs = dict(
        yg=sd((2, 64, FH), BF), yu=sd((2, 64, FH), BF), yd=sd((2, 64, FH), BF), oo=sd((64, 512), F32),
        oq=sd((64, 512), F32), ok=sd((64, HD), F32), ov=sd((64, HD), F32),
        res=sd((rows, d), BF), gtok=sd((rows, d), BF), dg1=sd((1, 64), F32), dg2=sd((1, 64), F32),
        pg=sd(part, BF), pu=sd(part, BF), pd=sd(part, BF),
    )
    scr = dict(
        bl=v((4, rows, d), BF), bc=v((4, rows, d), BF), by=v((2, rows, d), BF), bt=v((2, rows // 2, d), BF),
        gm=v((4, rows, d), BF), gmid=v((rows, d), F32), gatt=v((n, 512), BF),
        dqkv=v((n, 640), BF), ak=v((n, 128), F32), av=v((n, 128), F32),
        po=v((2, 4, 4, 64, 512), BF), pq=v((2, 4, 4, 64, 640), BF),
        ap=v((4, rows, d), BF), arc=v((2, rows, d), BF), arh=v((rows, d), BF),
        yo=v((64, 512), BF), yq=v((64, 640), BF), dg=v((2, 64, 128), F32), dy=v((3, 2, 64, 128), F32),
        chunk=v((4, 2 * n, 256), BF), stage=v((4, 4, 64, FH), BF),
        csem=pltpu.SemaphoreType.DMA((4,)), ssem=pltpu.SemaphoreType.DMA((4,)), free=pltpu.SemaphoreType.REGULAR,
    )
    for k, w in (("g", FH), ("u", FH), ("d", FH), ("o", 512), ("q", 640)):
        scr["t" + k] = v((2, 2, 2, 64, w), BF)
        scr["r1" + k] = v((2, 2, 4, 64, w), BF)
        scr["r2" + k] = v((2, 3, 64, w), BF)
    for k in "gud":
        scr["l" + k] = v((2, 8, 64, FH), BF)
    sem = sems(132, 56)
    for k in LATE:
        u = vmem.pop(k)
        hbm["h_" + k] = u
        scr[k] = v(u.shape, u.dtype)
    names = list(hbm) + list(vmem) + list(outs) + list(scr) + ["send", "recv", "loc"]
    got = pl.pallas_call(
        functools.partial(m3_body, names),
        out_shape=list(outs.values()),
        in_specs=[ANY] * len(hbm) + [VM] * len(vmem),
        out_specs=[VM] * (len(outs) - 3) + [ANY] * 3,
        scratch_shapes=list(scr.values()) + sem,
        compiler_params=pltpu.CompilerParams(collective_id=3, has_side_effects=True, vmem_limit_bytes=62 << 20),
        name="attention_backward",
    )(*hbm.values(), *vmem.values())
    return dict(zip(outs, got))


def mm(l, r, dims=((1,), (0,))):
    return lax.dot_general(l, r, (dims, ((), ())), preferred_element_type=F32)


def final_body(yg, yu, yd, *refs):
    k = (len(refs) - 3) // 2
    for y, o in zip((yg, yu, yd), refs[k : k + 3]):
        rest = o.shape[1] - FH
        o[:, :FH] = y[0].astype(F32)
        o[:, FH:] = y[1, :, :rest].astype(F32)
    for i, o in zip(refs[:k], refs[k + 3 :]):
        o[...] = i[...]


def final(halves, others, ff):
    sd = jax.ShapeDtypeStruct
    return pl.pallas_call(
        final_body,
        out_shape=[sd((64, ff), F32)] * 3 + [sd(o.shape, o.dtype) for o in others],
        in_specs=[VM] * (3 + len(others)),
        out_specs=[VM] * (3 + len(others)),
        name="final",
    )(*halves, *others)


def per_device(
    tokens_in, cotangent, seq_ids, block_ids, positions, attn_gain, ffn_gain,
    w_query, w_key, w_value, w_out, w_gate, w_up, w_down,
):
    rows, d = tokens_in.shape
    n = seq_ids.shape[0]
    weights = (w_query, w_key, w_value, w_out.T, w_gate, w_up, w_down.T)
    g_a, g_f = attn_gain.reshape(1, -1), ffn_gain.reshape(1, -1)
    xf, mid, gains, xn, q, kv4, att, wqkv, wot, cos, sin, bias_t, cot, wg, wu, wdt = m1(
        tokens_in, cotangent, weights, g_a, g_f, seq_ids, block_ids, positions
    )
    cot = cot.reshape(2 * n, d)
    wg, wu, wdt = (w.reshape(d, FH) for w in (wg, wu, wdt))
    xf = xf.reshape(2 * n, d)
    gate = mm(xf, wg)
    up = mm(xf, wu)
    sig = jax.nn.sigmoid(gate)
    silu = gate * sig
    hid = (silu * up).astype(BF)
    gh = mm(cot, wdt)
    dgate = (gh * up * (sig * (1.0 + gate * (1.0 - sig)))).astype(BF)
    dup = (gh * silu).astype(BF)
    fback = (mm(dgate, wg, NT) + mm(dup, wu, NT)).astype(BF).reshape(2, 4, rows, d)
    fout = mm(hid, wdt, NT).astype(BF).reshape(2, 4, rows, d)
    out = m3(
        dict(fback=fback, fout=fout, xf=xf, call=cot),
        dict(
            hid=hid, dgate=dgate, dup=dup, mid=mid, cot=cotangent, tok=tokens_in, gains=gains, xn=xn, q=q, kv4=kv4,
            att=att, wq=wqkv, wo=wot, cos=cos, sin=sin, bias=bias_t,
            w_q=w_query, w_k=w_key, w_v=w_value, w_g=w_gate, w_u=w_up, g_a=g_a, g_f=g_f,
        ),
        (rows, d),
    )
    keep = ("res", "gtok", "dg1", "dg2", "oq", "ok", "ov", "oo")
    og, ou, od, res, gtok, dg1, dg2, oq, ok, ov, oo = final(
        [out[k] for k in ("yg", "yu", "yd")], [out[k] for k in keep], w_gate.shape[1]
    )
    return (res, gtok, dg1.reshape(-1), dg2.reshape(-1), oq, ok, ov, oo.T, og, ou, od.T)


def solution(mesh):
    both, dp, cols, rows = P(("dp", "tensor"), None), P("dp"), P("dp", "tensor"), P("tensor", "dp")
    return jax.shard_map(
        per_device,
        mesh=mesh,
        in_specs=(both, both, dp, dp, dp, dp, dp, cols, cols, cols, rows, cols, cols, rows),
        out_specs=(both, both, dp, dp, cols, cols, cols, rows, cols, cols, rows),
        check_vma=False,
    )
```

profile of v0, /device:TPU:1, one launch (start us, length us, event | category | flops | bytes accessed | tf_op | source)
XLA Modules:
  0.0 259.3 jit_solution(13338615290084504812)
XLA Ops:
  0.6 107.1 %attention_forward.1 = (bf16[2,4,128,2048]{3,2,1,0:T(8,128)(2,1)}, f32[128,2048]{1,0:T(8,128)}, f32[8,2048]{1,0:T(8,128)}, bf16[512,2048]{1,0:T(8,128)(2,1)}, bf...) custom-call(bf16[128,2048]{1,0:T(8,128)(2,1)} %refs_16_.1, ...), custom_call_target="tpu_custom_call" | custom-call | tf_op jit(solution)/shard_map/attention_forward/pallas_call | solution.py:434
  107.8 0.0 copy-start.1
  107.8 0.0 copy-start.5
  107.8 6.5 %fusion.2 = f32[1024,768]{1,0:T(8,128)S(1)} fusion(bf16[1024,2048]{1,0:T(8,128)(2,1)} %bitcast.30, bf16[2048,768]{1,0:T(8,128)(2,1)} %bitcast.50), kind=kOutput, calls=%fused_computation.8 | convolution fusion | flops 3221225472 | bytes 10485760 | tf_op jit(solution)/shard_map/dot_general | solution.py:872
  114.3 0.0 copy-done.1
  114.3 0.0 copy-done.5
  114.3 0.0 copy-start
  114.3 0.0 copy-start.6
  114.3 3.4 %fusion.1 = f32[1024,768]{1,0:T(8,128)S(1)} fusion(bf16[1024,2048]{1,0:T(8,128)(2,1)S(1)} %bitcast.34, bf16[2048,768]{1,0:T(8,128)(2,1)S(1)} %bitcast.46), kind=kOutput, calls=%fused_computation.7 | convolution fusion | flops 3221225472 | bytes 10485760 | tf_op jit(solution)/shard_map/dot_general | solution.py:872
  117.8 0.0 copy-done
  117.8 0.0 copy-done.6
  117.8 0.0 copy-start.7
  117.8 4.5 %multiply_convert_fusion = (bf16[1024,768]{1,0:T(8,128)(2,1)S(1)}, bf16[1024,768]{1,0:T(8,128)(2,1)S(1)}, bf16[1024,768]{1,0:T(8,128)(2,1)S(1)}) fusion(f32[1024,768]{1,0:T(8,128)S(1)} %fusion.2, f32[1024,768]{1,0:T(8,128)S(1)} %fusion.1, bf16[1024,2048]{1,0:T(8,128)(2,1)S(1)} %bitcast.32, bf16[2048,768]{1,0:T(8,128)(2,1)S(1)} %bitcast.48), kind=kOutput, calls=%fused_computation.2 | convolution fusion | flops 3233021952 | bytes 18350080 | tf_op jit(solution)/shard_map/dot_general | solution.py:872
  122.3 0.0 copy-start.3
  122.3 0.0 copy-start.4
  122.4 0.0 copy-start.2
  122.4 0.0 copy-done.7
  122.4 3.4 %fusion.3 = f32[1024,2048]{1,0:T(8,128)S(1)} fusion(bf16[1024,768]{1,0:T(8,128)(2,1)S(1)} %get-tuple-element.88.refs_5_, bf16[2048,768]{1,0:T(8,128)(2,1)S(1)} %bitcast.51), kind=kOutput, calls=%fused_computation.9 | convolution fusion | flops 3221225472 | bytes 13107200 | tf_op jit(solution)/shard_map/dot_general | solution.py:872
  125.8 0.0 copy-done.3
  125.8 0.0 copy-done.4
  125.8 5.1 %add_convert_fusion = bf16[1024,2048]{1,0:T(8,128)(2,1)} fusion(f32[1024,2048]{1,0:T(8,128)S(1)} %fusion.3, bf16[1024,768]{1,0:T(8,128)(2,1)S(1)} %get-tuple-element.89.refs_6_, bf16[2048,768]{1,0:T(8,128)(2,1)S(1)} %bitcast.49), kind=kOutput, calls=%fused_computation | convolution fusion | flops 3225419776 | bytes 17301504 | tf_op jit(solution)/shard_map/dot_general | solution.py:872
  130.9 0.0 copy-done.2
  130.9 5.0 %convolution_convert_fusion = bf16[1024,2048]{1,0:T(8,128)(2,1)} fusion(bf16[1024,768]{1,0:T(8,128)(2,1)S(1)} %get-tuple-element.87.refs_4_, bf16[2048,768]{1,0:T(8,128)(2,1)S(1)} %bitcast.47), kind=kOutput, calls=%fused_computation.1 | convolution fusion | flops 3223322624 | bytes 8912896 | tf_op jit(solution)/shard_map/dot_general | solution.py:872
  135.9 120.3 %attention_backward.1 = (bf16[2,64,768]{2,1,0:T(8,128)(2,1)}, bf16[2,64,768]{2,1,0:T(8,128)(2,1)}, bf16[2,64,768]{2,1,0:T(8,128)(2,1)}, f32[64,512]{1,0:T(8,128)...) custom-call(bf16[2,4,128,2048]{3,2,1,0:T(8,128)(2,1)} %bitcast.35, ...), custom_call_target="tpu_custom_call" | custom-call | tf_op jit(solution)/shard_map/attention_backward/pallas_call | solution.py:859
  256.2 3.0 %final.1 = (f32[64,1408]{1,0:T(8,128)}, f32[64,1408]{1,0:T(8,128)}, f32[64,1408]{1,0:T(8,128)}, bf16[128,2048]{1,0:T(8,128)(2,1)}, bf16[128,2048]{1,0:T(8,128)(2...) custom-call(bf16[2,64,768]{2,1,0:T(8,128)(2,1)} %get-tuple-element.6, ...), custom_call_target="tpu_custom_call" | custom-call | tf_op jit(solution)/shard_map/final/pallas_call | solution.py:887
Async XLA Ops:
  107.8 6.5 %copy-start.1 = (bf16[2,4,128,2048]{3,2,1,0:T(8,128)(2,1)S(1)}, bf16[2,4,128,2048]{3,2,1,0:T(8,128)(2,1)}, u32[]{:S(2)}) copy-start(bf16[2,4,128,2048]{3,2,1,0:T(8,128)(2,1)} %get-tuple-element.49) | copy-start | bytes 12582916
  107.8 6.5 %copy-start.5 = (bf16[2,4,4,64,768]{4,3,2,1,0:T(8,128)(2,1)S(1)}, bf16[2,4,4,64,768]{4,3,2,1,0:T(8,128)(2,1)}, u32[]{:S(2)}) copy-start(bf16[2,4,4,64,768]{4,3,2,1,0:T(8,128)(2,1)} %get-tuple-element.50) | copy-start | bytes 9437188
  114.3 3.5 %copy-start = (bf16[2,4,128,2048]{3,2,1,0:T(8,128)(2,1)S(1)}, bf16[2,4,128,2048]{3,2,1,0:T(8,128)(2,1)}, u32[]{:S(2)}) copy-start(bf16[2,4,128,2048]{3,2,1,0:T(8,128)(2,1)} %get-tuple-element.51) | copy-start | bytes 12582916
  114.3 3.5 %copy-start.6 = (bf16[2,4,4,64,768]{4,3,2,1,0:T(8,128)(2,1)S(1)}, bf16[2,4,4,64,768]{4,3,2,1,0:T(8,128)(2,1)}, u32[]{:S(2)}) copy-start(bf16[2,4,4,64,768]{4,3,2,1,0:T(8,128)(2,1)} %get-tuple-element.52) | copy-start | bytes 9437188
  117.8 4.6 %copy-start.7 = (bf16[2,4,4,64,768]{4,3,2,1,0:T(8,128)(2,1)S(1)}, bf16[2,4,4,64,768]{4,3,2,1,0:T(8,128)(2,1)}, u32[]{:S(2)}) copy-start(bf16[2,4,4,64,768]{4,3,2,1,0:T(8,128)(2,1)} %get-tuple-element.53) | copy-start | bytes 9437188
  122.3 3.5 %copy-start.3 = (bf16[1024,768]{1,0:T(8,128)(2,1)}, bf16[1024,768]{1,0:T(8,128)(2,1)S(1)}, u32[]{:S(2)}) copy-start(bf16[1024,768]{1,0:T(8,128)(2,1)S(1)} %get-tuple-element.88.refs_5_) | copy-start | bytes 4718596
  122.3 3.5 %copy-start.4 = (bf16[1024,768]{1,0:T(8,128)(2,1)}, bf16[1024,768]{1,0:T(8,128)(2,1)S(1)}, u32[]{:S(2)}) copy-start(bf16[1024,768]{1,0:T(8,128)(2,1)S(1)} %get-tuple-element.89.refs_6_) | copy-start | bytes 4718596
  122.4 8.5 %copy-start.2 = (bf16[1024,768]{1,0:T(8,128)(2,1)}, bf16[1024,768]{1,0:T(8,128)(2,1)S(1)}, u32[]{:S(2)}) copy-start(bf16[1024,768]{1,0:T(8,128)(2,1)S(1)} %get-tuple-element.87.refs_4_) | copy-start | bytes 4718596
where the time goes:
time: 260 us; the launch traced here: 259 us
  Pallas kernels  230 us (88%)
  matrix products  27.9 us (11%)
    pallas_call x1, Pallas kernels, m3(): pl.pallas_call(functools.partial(m3_body, names), out_shape=list(outs.val...  120 us
    pallas_call x1, Pallas kernels, m1(): pl.pallas_call(m1_body, out_shape=[sd((2, 4, rows, d), BF), sd((rows, d),...  107 us
    dot_general x6, matrix products, mm(): return lax.dot_general(l, r, (dims, ((), ())), preferred_element_type=F32)  27.9 us

commit v1 on v0

--- a/solution.py
+++ b/solution.py
@@ -435,7 +435,7 @@
         m1_body,
         out_shape=[sd((2, 4, rows, d), BF), sd((rows, d), F32), sd((8, d), F32)]
         + [sd(*k) for k in kept] + [sd((2, 4, rows, d), BF)] + ffn,
-        in_specs=[ANY] * 2 + [VM] * 13,
+        in_specs=[ANY] + [VM] * 14,
         out_specs=[VM] * 3 + [ANY] * 13,
         scratch_shapes=[v(*k) for k in kept] + [
             v((64, 640), BF), v((3, 2, 64, FH), BF), v((8, 128), F32),
@@ -626,7 +626,7 @@
             save(i, w, n * (i % 2) + w).wait()
 
 
-SOON = ("hid", "dgate", "dup")
+SOON = ("hid", "dgate", "dup", "cot", "mid")
 LATE = SOON + ("xn", "q", "kv4", "att", "wq", "wo", "cos", "sin", "bias", "tok", "w_q", "w_k", "w_v", "w_g", "w_u")
 
 
@@ -659,6 +659,8 @@
     back.mid()
     ffn[1].stage_one()
     ffn[2].stage_one()
+    soon[3].wait()
+    soon[4].wait()
     back.arrived()
     gm, gmid = r["gm"], r["gmid"]
 

time: 260 us -> 260 us (level)
  no operation moved by 1% of the time
where the time goes in v1:
time: 260 us; the launch traced here: 259 us
  Pallas kernels  230 us (88%)
  matrix products  27.9 us (11%)
    pallas_call x1, Pallas kernels, m3(): pl.pallas_call(functools.partial(m3_body, names), out_shape=list(outs.val...  120 us
    pallas_call x1, Pallas kernels, m1(): pl.pallas_call(m1_body, out_shape=[sd((2, 4, rows, d), BF), sd((rows, d),...  107 us
    dot_general x6, matrix products, mm(): return lax.dot_general(l, r, (dims, ((), ())), preferred_element_type=F32)  27.9 us

profile of v1, /device:TPU:1, one launch (start us, length us, event | category | flops | bytes accessed | tf_op | source)
XLA Modules:
  0.0 259.4 jit_solution(11117450697365982848)
XLA Ops:
  0.6 107.3 %attention_forward.1 = (bf16[2,4,128,2048]{3,2,1,0:T(8,128)(2,1)}, f32[128,2048]{1,0:T(8,128)}, f32[8,2048]{1,0:T(8,128)}, bf16[512,2048]{1,0:T(8,128)(2,1)}, bf...) custom-call(bf16[128,2048]{1,0:T(8,128)(2,1)} %refs_18_.1, ...), custom_call_target="tpu_custom_call" | custom-call | tf_op jit(solution)/shard_map/attention_forward/pallas_call | solution.py:434
  107.9 0.0 copy-start.1
  107.9 0.0 copy-start.5
  107.9 6.5 %fusion.2 = f32[1024,768]{1,0:T(8,128)S(1)} fusion(bf16[1024,2048]{1,0:T(8,128)(2,1)} %bitcast.30, bf16[2048,768]{1,0:T(8,128)(2,1)} %bitcast.50), kind=kOutput, calls=%fused_computation.8 | convolution fusion | flops 3221225472 | bytes 10485760 | tf_op jit(solution)/shard_map/dot_general | solution.py:874
  114.4 0.0 copy-done.1
  114.4 0.0 copy-done.5
  114.4 0.0 copy-start
  114.4 0.0 copy-start.6
  114.4 3.4 %fusion.1 = f32[1024,768]{1,0:T(8,128)S(1)} fusion(bf16[1024,2048]{1,0:T(8,128)(2,1)S(1)} %bitcast.34, bf16[2048,768]{1,0:T(8,128)(2,1)S(1)} %bitcast.46), kind=kOutput, calls=%fused_computation.7 | convolution fusion | flops 3221225472 | bytes 10485760 | tf_op jit(solution)/shard_map/dot_general | solution.py:874
  117.9 0.0 copy-done
  117.9 0.0 copy-done.6
  117.9 0.0 copy-start.7
  117.9 4.5 %multiply_convert_fusion = (bf16[1024,768]{1,0:T(8,128)(2,1)S(1)}, bf16[1024,768]{1,0:T(8,128)(2,1)S(1)}, bf16[1024,768]{1,0:T(8,128)(2,1)S(1)}) fusion(f32[1024,768]{1,0:T(8,128)S(1)} %fusion.2, f32[1024,768]{1,0:T(8,128)S(1)} %fusion.1, bf16[1024,2048]{1,0:T(8,128)(2,1)S(1)} %bitcast.32, bf16[2048,768]{1,0:T(8,128)(2,1)S(1)} %bitcast.48), kind=kOutput, calls=%fused_computation.2 | convolution fusion | flops 3233021952 | bytes 18350080 | tf_op jit(solution)/shard_map/dot_general | solution.py:874
  122.5 0.0 copy-start.3
  122.5 0.0 copy-start.4
  122.5 0.0 copy-start.2
  122.5 0.0 copy-done.7
  122.5 3.4 %fusion.3 = f32[1024,2048]{1,0:T(8,128)S(1)} fusion(bf16[1024,768]{1,0:T(8,128)(2,1)S(1)} %get-tuple-element.88.refs_5_, bf16[2048,768]{1,0:T(8,128)(2,1)S(1)} %bitcast.51), kind=kOutput, calls=%fused_computation.9 | convolution fusion | flops 3221225472 | bytes 13107200 | tf_op jit(solution)/shard_map/dot_general | solution.py:874
  125.9 0.0 copy-done.3
  126.0 0.0 copy-done.4
  126.0 5.1 %add_convert_fusion = bf16[1024,2048]{1,0:T(8,128)(2,1)} fusion(f32[1024,2048]{1,0:T(8,128)S(1)} %fusion.3, bf16[1024,768]{1,0:T(8,128)(2,1)S(1)} %get-tuple-element.89.refs_6_, bf16[2048,768]{1,0:T(8,128)(2,1)S(1)} %bitcast.49), kind=kOutput, calls=%fused_computation | convolution fusion | flops 3225419776 | bytes 17301504 | tf_op jit(solution)/shard_map/dot_general | solution.py:874
  131.0 0.0 copy-done.2
  131.0 5.0 %convolution_convert_fusion = bf16[1024,2048]{1,0:T(8,128)(2,1)} fusion(bf16[1024,768]{1,0:T(8,128)(2,1)S(1)} %get-tuple-element.87.refs_4_, bf16[2048,768]{1,0:T(8,128)(2,1)S(1)} %bitcast.47), kind=kOutput, calls=%fused_computation.1 | convolution fusion | flops 3223322624 | bytes 8912896 | tf_op jit(solution)/shard_map/dot_general | solution.py:874
  136.0 120.2 %attention_backward.1 = (bf16[2,64,768]{2,1,0:T(8,128)(2,1)}, bf16[2,64,768]{2,1,0:T(8,128)(2,1)}, bf16[2,64,768]{2,1,0:T(8,128)(2,1)}, f32[64,512]{1,0:T(8,128)...) custom-call(bf16[2,4,128,2048]{3,2,1,0:T(8,128)(2,1)} %bitcast.35, ...), custom_call_target="tpu_custom_call" | custom-call | tf_op jit(solution)/shard_map/attention_backward/pallas_call | solution.py:861
  256.2 3.0 %final.1 = (f32[64,1408]{1,0:T(8,128)}, f32[64,1408]{1,0:T(8,128)}, f32[64,1408]{1,0:T(8,128)}, bf16[128,2048]{1,0:T(8,128)(2,1)}, bf16[128,2048]{1,0:T(8,128)(2...) custom-call(bf16[2,64,768]{2,1,0:T(8,128)(2,1)} %get-tuple-element.6, ...), custom_call_target="tpu_custom_call" | custom-call | tf_op jit(solution)/shard_map/final/pallas_call | solution.py:889
Async XLA Ops:
  107.9 6.5 %copy-start.1 = (bf16[2,4,128,2048]{3,2,1,0:T(8,128)(2,1)S(1)}, bf16[2,4,128,2048]{3,2,1,0:T(8,128)(2,1)}, u32[]{:S(2)}) copy-start(bf16[2,4,128,2048]{3,2,1,0:T(8,128)(2,1)} %get-tuple-element.49) | copy-start | bytes 12582916
  107.9 6.5 %copy-start.5 = (bf16[2,4,4,64,768]{4,3,2,1,0:T(8,128)(2,1)S(1)}, bf16[2,4,4,64,768]{4,3,2,1,0:T(8,128)(2,1)}, u32[]{:S(2)}) copy-start(bf16[2,4,4,64,768]{4,3,2,1,0:T(8,128)(2,1)} %get-tuple-element.50) | copy-start | bytes 9437188
  114.4 3.5 %copy-start = (bf16[2,4,128,2048]{3,2,1,0:T(8,128)(2,1)S(1)}, bf16[2,4,128,2048]{3,2,1,0:T(8,128)(2,1)}, u32[]{:S(2)}) copy-start(bf16[2,4,128,2048]{3,2,1,0:T(8,128)(2,1)} %get-tuple-element.51) | copy-start | bytes 12582916
  114.4 3.5 %copy-start.6 = (bf16[2,4,4,64,768]{4,3,2,1,0:T(8,128)(2,1)S(1)}, bf16[2,4,4,64,768]{4,3,2,1,0:T(8,128)(2,1)}, u32[]{:S(2)}) copy-start(bf16[2,4,4,64,768]{4,3,2,1,0:T(8,128)(2,1)} %get-tuple-element.52) | copy-start | bytes 9437188
  117.9 4.6 %copy-start.7 = (bf16[2,4,4,64,768]{4,3,2,1,0:T(8,128)(2,1)S(1)}, bf16[2,4,4,64,768]{4,3,2,1,0:T(8,128)(2,1)}, u32[]{:S(2)}) copy-start(bf16[2,4,4,64,768]{4,3,2,1,0:T(8,128)(2,1)} %get-tuple-element.53) | copy-start | bytes 9437188
  122.5 3.5 %copy-start.3 = (bf16[1024,768]{1,0:T(8,128)(2,1)}, bf16[1024,768]{1,0:T(8,128)(2,1)S(1)}, u32[]{:S(2)}) copy-start(bf16[1024,768]{1,0:T(8,128)(2,1)S(1)} %get-tuple-element.88.refs_5_) | copy-start | bytes 4718596
  122.5 3.5 %copy-start.4 = (bf16[1024,768]{1,0:T(8,128)(2,1)}, bf16[1024,768]{1,0:T(8,128)(2,1)S(1)}, u32[]{:S(2)}) copy-start(bf16[1024,768]{1,0:T(8,128)(2,1)S(1)} %get-tuple-element.89.refs_6_) | copy-start | bytes 4718596
  122.5 8.5 %copy-start.2 = (bf16[1024,768]{1,0:T(8,128)(2,1)}, bf16[1024,768]{1,0:T(8,128)(2,1)S(1)}, u32[]{:S(2)}) copy-start(bf16[1024,768]{1,0:T(8,128)(2,1)S(1)} %get-tuple-element.87.refs_4_) | copy-start | bytes 4718596
